TPU v7x, 256 devices: a whole 4x4x8 slice. The times are simulated.
256 devices in a mesh: row: 32 (over x, z_hi, y), col: 8 (over z_lo, core).
Axes of the slice: x: 4, y: 4, z: 8 (z_hi: 2, z_lo: 4; z = z_hi * 4 + z_lo), core: 2. Of those that a mesh axis runs over, the one named last changes fastest.
Arguments:
- coupling: float32 [24576, 24576], P('row', 'col'), may hold values from -1 to 5, as said below
- vectors: float32 [24576, 256], P(('row', 'col')), may hold values from -6 to 6
Outputs:
- filtered: float32 [24576, 256], P(('row', 'col'))
- gram: float32 [256, 256], replicated
Inputs may be any that keep to these rules, and one draw needn't show every extreme that they name: `coupling`: H, the operator with its column order restored, is symmetric.
All inputs are finite; a program needn't handle non-finite values.
Results may differ from a plain program's by a relative error of at most 0.0001.
Values sent between devices are 32-bit elements; how exact they have to be, the bound alone decides.
No kernel may reach another device: no remote copies, remote signals or barrier semaphores. Data moves between devices by JAX's collectives and lax.ppermute only.
A program may use at most 64 MiB of HBM per device.

v0:
```python
import jax
import jax.numpy as jnp
from jax import lax
from jax.sharding import PartitionSpec as P

ORDER = 24576
DEGREE = 6
filter_center = 2.75
filter_half = 1.75
filter_lower = 0.0


def on_device(coupling, vectors):

    def operate(current):
        partial_value = jnp.dot(
            coupling,
            lax.all_gather(current, "row", axis=0, tiled=True),
            precision=lax.Precision.HIGHEST,
            preferred_element_type=jnp.float32,
        )
        product = lax.psum_scatter(partial_value, "col", scatter_dimension=0, tiled=True)
        return product - filter_center * current

    sigma_first = filter_half / (filter_lower - filter_center)
    previous = vectors
    current = sigma_first / filter_half * operate(vectors)
    sigma_now = sigma_first
    for degree_index in range(DEGREE - 1):
        sigma_new = 1.0 / (2.0 / sigma_first - sigma_now)
        following = (
            2.0 * sigma_new / filter_half * operate(current) - sigma_now * sigma_new * previous
        )
        previous = current
        current = following
        sigma_now = sigma_new
    local_gram = jnp.dot(
        current.T, current, precision=lax.Precision.HIGHEST, preferred_element_type=jnp.float32
    )
    gram = lax.psum(local_gram, ("row", "col")) / ORDER
    return (current, gram)


def solution(mesh):
    return jax.shard_map(
        on_device,
        mesh=mesh,
        in_specs=(P("row", "col"), P(("row", "col"), None)),
        out_specs=(P(("row", "col"), None), P()),
        check_vma=False,
    )
```

profile of v0, /device:TPU:2, one launch (start us, length us, event | category | flops | bytes accessed | tf_op | source)
XLA Modules:
  0.0 1155.9 jit_solution(2117309607729727020)
XLA Ops:
  8.0 105.9 %all-gather.7.cloned.1.call-done = f32[3072,256]{1,0:T(8,128)} async-done(((f32[96,256]{1,0:T(8,128)}), f32[3072,256]{1,0:T(8,128)}) %all-gather.7.cloned.1.call-update) | async-done | bytes 3145744 | tf_op jit(solution)/shard_map/all_gather | solution.py:18
  113.9 11.4 fusion
  125.4 32.3 %reduce-scatter.7.cloned.1.call-done = f32[96,256]{1,0:T(8,128)} async-done(((f32[768,256]{1,0:T(8,128)}), f32[96,256]{1,0:T(8,128)}) %reduce-scatter.7.cloned.1.call-update) | async-done | bytes 98320 | tf_op jit(solution)/shard_map/reduce_scatter | solution.py:22
  159.4 100.7 %all-gather.9.cloned.1.call-done = f32[3072,256]{1,0:T(8,128)} async-done(((f32[96,256]{1,0:T(8,128)}), f32[3072,256]{1,0:T(8,128)}) %all-gather.9.cloned.1.call-update) | async-done | bytes 3145744 | tf_op jit(solution)/shard_map/all_gather | solution.py:18
  260.1 11.4 convolution_bitcast_fusion.4
  271.6 32.3 %reduce-scatter.9.cloned.1.call-done = f32[96,256]{1,0:T(8,128)} async-done(((f32[768,256]{1,0:T(8,128)}), f32[96,256]{1,0:T(8,128)}) %reduce-scatter.9.cloned.1.call-update) | async-done | bytes 98320 | tf_op jit(solution)/shard_map/reduce_scatter | solution.py:22
  303.9 1.6 multiply_subtract_fusion.4
  305.7 100.4 %all-gather.11.cloned.1.call-done = f32[3072,256]{1,0:T(8,128)} async-done(((f32[96,256]{1,0:T(8,128)}), f32[3072,256]{1,0:T(8,128)}) %all-gather.11.cloned.1.call-update) | async-done | bytes 3145744 | tf_op jit(solution)/shard_map/all_gather | solution.py:18
  406.1 11.4 convolution_bitcast_fusion.3
  417.7 32.3 %reduce-scatter.11.cloned.1.call-done = f32[96,256]{1,0:T(8,128)} async-done(((f32[768,256]{1,0:T(8,128)}), f32[96,256]{1,0:T(8,128)}) %reduce-scatter.11.cloned.1.call-update) | async-done | bytes 98320 | tf_op jit(solution)/shard_map/reduce_scatter | solution.py:22
  450.0 1.6 multiply_subtract_fusion.3
  451.6 100.7 %all-gather.13.cloned.1.call-done = f32[3072,256]{1,0:T(8,128)} async-done(((f32[96,256]{1,0:T(8,128)}), f32[3072,256]{1,0:T(8,128)}) %all-gather.13.cloned.1.call-update) | async-done | bytes 3145744 | tf_op jit(solution)/shard_map/all_gather | solution.py:18
  552.4 11.4 convolution_bitcast_fusion.2
  563.9 32.3 %reduce-scatter.13.cloned.1.call-done = f32[96,256]{1,0:T(8,128)} async-done(((f32[768,256]{1,0:T(8,128)}), f32[96,256]{1,0:T(8,128)}) %reduce-scatter.13.cloned.1.call-update) | async-done | bytes 98320 | tf_op jit(solution)/shard_map/reduce_scatter | solution.py:22
  596.2 1.6 multiply_subtract_fusion.2
  598.1 100.5 %all-gather.15.cloned.1.call-done = f32[3072,256]{1,0:T(8,128)} async-done(((f32[96,256]{1,0:T(8,128)}), f32[3072,256]{1,0:T(8,128)}) %all-gather.15.cloned.1.call-update) | async-done | bytes 3145744 | tf_op jit(solution)/shard_map/all_gather | solution.py:18
  698.6 11.4 convolution_bitcast_fusion.1
  710.2 32.3 %reduce-scatter.15.cloned.1.call-done = f32[96,256]{1,0:T(8,128)} async-done(((f32[768,256]{1,0:T(8,128)}), f32[96,256]{1,0:T(8,128)}) %reduce-scatter.15.cloned.1.call-update) | async-done | bytes 98320 | tf_op jit(solution)/shard_map/reduce_scatter | solution.py:22
  742.5 1.6 multiply_subtract_fusion.1
  744.1 100.7 %all-gather.17.cloned.1.call-done = f32[3072,256]{1,0:T(8,128)} async-done(((f32[96,256]{1,0:T(8,128)}), f32[3072,256]{1,0:T(8,128)}) %all-gather.17.cloned.1.call-update) | async-done | bytes 3145744 | tf_op jit(solution)/shard_map/all_gather | solution.py:18
  844.8 11.4 convolution_bitcast_fusion
  856.3 32.3 %reduce-scatter.17.cloned.1.call-done = f32[96,256]{1,0:T(8,128)} async-done(((f32[768,256]{1,0:T(8,128)}), f32[96,256]{1,0:T(8,128)}) %reduce-scatter.17.cloned.1.call-update) | async-done | bytes 98320 | tf_op jit(solution)/shard_map/reduce_scatter | solution.py:22
  890.8 257.0 %all-reduce.2.cloned.1.call-done = f32[256,256]{1,0:T(8,128)} async-done(((f32[256,256]{1,0:T(8,128)}), f32[256,256]{1,0:T(8,128)}) %all-reduce.2.cloned.1.call-update) | async-done | bytes 262160 | tf_op jit(solution)/shard_map/psum | solution.py:40
  1147.7 1.7 broadcast_multiply_fusion
  (43 shorter events, 5.4 us)
Async XLA Ops:
  7.2 106.7 %all-gather.7.cloned.1.call-start = ((), (), s32[]{:S(2)}) async-start(), calls=%async_computation.6 | async-start | bytes 3244032 | tf_op jit(solution)/shard_map/all_gather | solution.py:18
  7.9 149.8 %copy-start = (f32[96,256]{1,0:T(8,128)S(1)}, f32[96,256]{1,0:T(8,128)}, u32[]{:S(2)}) copy-start(f32[96,256]{1,0:T(8,128)} %param.3) | copy-start | bytes 294916
  7.9 149.8 %reduce-scatter.7.cloned.1.call-start = ((), (), s32[]{:S(2)}) async-start(), calls=%async_computation.7 | async-start | bytes 884736 | tf_op jit(solution)/shard_map/reduce_scatter | solution.py:22
  125.3 134.7 %all-gather.9.cloned.1.call-start = ((), (), s32[]{:S(2)}) async-start(), calls=%async_computation.8 | async-start | bytes 3244032 | tf_op jit(solution)/shard_map/all_gather | solution.py:18
  159.3 144.6 %copy-start.6 = (f32[96,256]{1,0:T(8,128)S(1)}, f32[96,256]{1,0:T(8,128)}, u32[]{:S(2)}) copy-start(f32[96,256]{1,0:T(8,128)} %reduce-scatter.7.cloned.1.call-done) | copy-start | bytes 294916
  159.3 144.6 %reduce-scatter.9.cloned.1.call-start = ((), (), s32[]{:S(2)}) async-start(), calls=%async_computation.9 | async-start | bytes 884736 | tf_op jit(solution)/shard_map/reduce_scatter | solution.py:22
  271.5 134.6 %all-gather.11.cloned.1.call-start = ((), (), s32[]{:S(2)}) async-start(), calls=%async_computation.10 | async-start | bytes 3244032 | tf_op jit(solution)/shard_map/all_gather | solution.py:18
  305.5 144.5 %copy-start.3 = (f32[96,256]{1,0:T(8,128)S(1)}, f32[96,256]{1,0:T(8,128)}, u32[]{:S(2)}) copy-start(f32[96,256]{1,0:T(8,128)} %multiply_subtract_fusion.4) | copy-start | bytes 294916
  305.5 144.5 %reduce-scatter.11.cloned.1.call-start = ((), (), s32[]{:S(2)}) async-start(), calls=%async_computation.11 | async-start | bytes 884736 | tf_op jit(solution)/shard_map/reduce_scatter | solution.py:22
  417.6 134.8 %all-gather.13.cloned.1.call-start = ((), (), s32[]{:S(2)}) async-start(), calls=%async_computation.12 | async-start | bytes 3244032 | tf_op jit(solution)/shard_map/all_gather | solution.py:18
  451.6 144.6 %copy-start.1 = (f32[96,256]{1,0:T(8,128)S(1)}, f32[96,256]{1,0:T(8,128)}, u32[]{:S(2)}) copy-start(f32[96,256]{1,0:T(8,128)} %multiply_subtract_fusion.3) | copy-start | bytes 294916
  451.6 144.6 %reduce-scatter.13.cloned.1.call-start = ((), (), s32[]{:S(2)}) async-start(), calls=%async_computation.13 | async-start | bytes 884736 | tf_op jit(solution)/shard_map/reduce_scatter | solution.py:22
  563.8 134.8 %all-gather.15.cloned.1.call-start = ((), (), s32[]{:S(2)}) async-start(), calls=%async_computation.14 | async-start | bytes 3244032 | tf_op jit(solution)/shard_map/all_gather | solution.py:18
  597.8 144.7 %copy-start.2 = (f32[96,256]{1,0:T(8,128)S(1)}, f32[96,256]{1,0:T(8,128)}, u32[]{:S(2)}) copy-start(f32[96,256]{1,0:T(8,128)} %multiply_subtract_fusion.2) | copy-start | bytes 294916
  597.8 144.7 %reduce-scatter.15.cloned.1.call-start = ((), (), s32[]{:S(2)}) async-start(), calls=%async_computation.15 | async-start | bytes 884736 | tf_op jit(solution)/shard_map/reduce_scatter | solution.py:22
  710.1 134.7 %all-gather.17.cloned.1.call-start = ((), (), s32[]{:S(2)}) async-start(), calls=%async_computation.16 | async-start | bytes 3244032 | tf_op jit(solution)/shard_map/all_gather | solution.py:18
  744.1 144.6 %copy-start.5 = (f32[96,256]{1,0:T(8,128)S(1)}, f32[96,256]{1,0:T(8,128)}, u32[]{:S(2)}) copy-start(f32[96,256]{1,0:T(8,128)} %multiply_subtract_fusion.1) | copy-start | bytes 294916
  744.1 144.6 %reduce-scatter.17.cloned.1.call-start = ((), (), s32[]{:S(2)}) async-start(), calls=%async_computation.17 | async-start | bytes 884736 | tf_op jit(solution)/shard_map/reduce_scatter | solution.py:22
  856.3 291.4 %all-reduce.2.cloned.1.call-start = ((), (), s32[]{:S(2)}) async-start(), calls=%async_computation.18 | async-start | bytes 524288 | tf_op jit(solution)/shard_map/psum | solution.py:40
  889.6 259.8 %copy-start.4 = (f32[96,256]{1,0:T(8,128)}, f32[96,256]{1,0:T(8,128)S(1)}, u32[]{:S(2)}) copy-start(f32[96,256]{1,0:T(8,128)S(1)} %multiply_subtract_fusion) | copy-start | bytes 294916
Sparse Core Ops, SparseCore 0:
  11.4 102.4 all-gather.6
  125.4 32.2 reduce-scatter.6
  161.7 98.3 all-gather.8
  271.6 32.2 reduce-scatter.8
  307.7 98.3 all-gather.10
  417.7 32.2 reduce-scatter.10
  454.0 98.3 all-gather.12
  564.0 32.2 reduce-scatter.12
  600.2 98.3 all-gather.14
  710.2 32.2 reduce-scatter.14
  746.5 98.3 all-gather.16
  856.4 32.2 reduce-scatter.16
  894.7 252.9 all-reduce.1
where the time goes:
time: 1160 us
  waiting for transfers between devices  1060 us (91%)
  matrix products  69.7 us (6%)
  between operations  14 us (1%)
    all_gather x6, waiting for transfers between devices, operate(): lax.all_gather(current, 'row', axis=0, tiled=True)  609 us
    psum x1, waiting for transfers between devices, on_device(): gram = lax.psum(local_gram, ('row', 'col')) / ORDER  257 us
    reduce_scatter x6, waiting for transfers between devices, operate(): lax.psum_scatter(partial_value, 'col', scatter_dimension=0, tiled=True)  194 us
    dot_general x6, matrix products, operate(): jnp.dot(coupling, lax.all_gather(current, 'row', axis=0, tiled=True), pre...  68.6 us
  transfers between devices with their start and end apart: 13, of which 13 were waited for; matrix products, arithmetic and copies ran while one was open for 0% of the time, Pallas kernels for 0%

commit v1 on v0

--- a/solution.py
+++ b/solution.py
@@ -37,7 +37,7 @@
     local_gram = jnp.dot(
         current.T, current, precision=lax.Precision.HIGHEST, preferred_element_type=jnp.float32
     )
-    gram = lax.psum(local_gram, ("row", "col")) / ORDER
+    gram = lax.psum(lax.psum(local_gram, "row"), "col") / ORDER
     return (current, gram)
 
 

time: 1160 us -> 1400 us (1.21)
  waiting for transfers between devices: 1060 us -> 1300 us
    psum x1 -> x2, waiting for transfers between devices: 257 us -> 501 us  [on_device(): gram = lax.psum(lax.psum(local_gram, 'row'), 'col') / ORDER]
  transfers between devices with their start and end apart: 13 -> 14, of which waited for: 13 -> 14; matrix products, arithmetic and copies ran while one was open for 0% -> 0% of each run, Pallas kernels for 0% -> 0%
where the time goes in v1:
time: 1400 us
  waiting for transfers between devices  1300 us (93%)
  matrix products  69.7 us (5%)
  between operations  14 us (1%)
    all_gather x6, waiting for transfers between devices, operate(): lax.all_gather(current, 'row', axis=0, tiled=True)  609 us
    psum x2, waiting for transfers between devices, on_device(): gram = lax.psum(lax.psum(local_gram, 'row'), 'col') / ORDER  501 us
    reduce_scatter x6, waiting for transfers between devices, operate(): lax.psum_scatter(partial_value, 'col', scatter_dimension=0, tiled=True)  194 us
    dot_general x6, matrix products, operate(): jnp.dot(coupling, lax.all_gather(current, 'row', axis=0, tiled=True), pre...  68.6 us
  transfers between devices with their start and end apart: 14, of which 14 were waited for; matrix products, arithmetic and copies ran while one was open for 0% of the time, Pallas kernels for 0%

profile of v1, /device:TPU:2, one launch (start us, length us, event | category | flops | bytes accessed | tf_op | source)
XLA Modules:
  0.0 1399.6 jit_solution(2903275294222887304)
XLA Ops:
  8.0 105.9 %all-gather.7.cloned.1.call-done = f32[3072,256]{1,0:T(8,128)} async-done(((f32[96,256]{1,0:T(8,128)}), f32[3072,256]{1,0:T(8,128)}) %all-gather.7.cloned.1.call-update) | async-done | bytes 3145744 | tf_op jit(solution)/shard_map/all_gather | solution.py:18
  113.9 11.4 fusion
  125.4 32.3 %reduce-scatter.7.cloned.1.call-done = f32[96,256]{1,0:T(8,128)} async-done(((f32[768,256]{1,0:T(8,128)}), f32[96,256]{1,0:T(8,128)}) %reduce-scatter.7.cloned.1.call-update) | async-done | bytes 98320 | tf_op jit(solution)/shard_map/reduce_scatter | solution.py:22
  159.4 100.7 %all-gather.9.cloned.1.call-done = f32[3072,256]{1,0:T(8,128)} async-done(((f32[96,256]{1,0:T(8,128)}), f32[3072,256]{1,0:T(8,128)}) %all-gather.9.cloned.1.call-update) | async-done | bytes 3145744 | tf_op jit(solution)/shard_map/all_gather | solution.py:18
  260.1 11.4 convolution_bitcast_fusion.4
  271.6 32.3 %reduce-scatter.9.cloned.1.call-done = f32[96,256]{1,0:T(8,128)} async-done(((f32[768,256]{1,0:T(8,128)}), f32[96,256]{1,0:T(8,128)}) %reduce-scatter.9.cloned.1.call-update) | async-done | bytes 98320 | tf_op jit(solution)/shard_map/reduce_scatter | solution.py:22
  303.9 1.6 multiply_subtract_fusion.4
  305.7 100.4 %all-gather.11.cloned.1.call-done = f32[3072,256]{1,0:T(8,128)} async-done(((f32[96,256]{1,0:T(8,128)}), f32[3072,256]{1,0:T(8,128)}) %all-gather.11.cloned.1.call-update) | async-done | bytes 3145744 | tf_op jit(solution)/shard_map/all_gather | solution.py:18
  406.1 11.4 convolution_bitcast_fusion.3
  417.7 32.3 %reduce-scatter.11.cloned.1.call-done = f32[96,256]{1,0:T(8,128)} async-done(((f32[768,256]{1,0:T(8,128)}), f32[96,256]{1,0:T(8,128)}) %reduce-scatter.11.cloned.1.call-update) | async-done | bytes 98320 | tf_op jit(solution)/shard_map/reduce_scatter | solution.py:22
  450.0 1.6 multiply_subtract_fusion.3
  451.6 100.7 %all-gather.13.cloned.1.call-done = f32[3072,256]{1,0:T(8,128)} async-done(((f32[96,256]{1,0:T(8,128)}), f32[3072,256]{1,0:T(8,128)}) %all-gather.13.cloned.1.call-update) | async-done | bytes 3145744 | tf_op jit(solution)/shard_map/all_gather | solution.py:18
  552.4 11.4 convolution_bitcast_fusion.2
  563.9 32.3 %reduce-scatter.13.cloned.1.call-done = f32[96,256]{1,0:T(8,128)} async-done(((f32[768,256]{1,0:T(8,128)}), f32[96,256]{1,0:T(8,128)}) %reduce-scatter.13.cloned.1.call-update) | async-done | bytes 98320 | tf_op jit(solution)/shard_map/reduce_scatter | solution.py:22
  596.2 1.6 multiply_subtract_fusion.2
  598.1 100.5 %all-gather.15.cloned.1.call-done = f32[3072,256]{1,0:T(8,128)} async-done(((f32[96,256]{1,0:T(8,128)}), f32[3072,256]{1,0:T(8,128)}) %all-gather.15.cloned.1.call-update) | async-done | bytes 3145744 | tf_op jit(solution)/shard_map/all_gather | solution.py:18
  698.6 11.4 convolution_bitcast_fusion.1
  710.2 32.3 %reduce-scatter.15.cloned.1.call-done = f32[96,256]{1,0:T(8,128)} async-done(((f32[768,256]{1,0:T(8,128)}), f32[96,256]{1,0:T(8,128)}) %reduce-scatter.15.cloned.1.call-update) | async-done | bytes 98320 | tf_op jit(solution)/shard_map/reduce_scatter | solution.py:22
  744.1 100.7 %all-gather.17.cloned.1.call-done = f32[3072,256]{1,0:T(8,128)} async-done(((f32[96,256]{1,0:T(8,128)}), f32[3072,256]{1,0:T(8,128)}) %all-gather.17.cloned.1.call-update) | async-done | bytes 3145744 | tf_op jit(solution)/shard_map/all_gather | solution.py:18
  844.8 11.4 convolution_bitcast_fusion
  856.3 32.3 %reduce-scatter.17.cloned.1.call-done = f32[96,256]{1,0:T(8,128)} async-done(((f32[768,256]{1,0:T(8,128)}), f32[96,256]{1,0:T(8,128)}) %reduce-scatter.17.cloned.1.call-update) | async-done | bytes 98320 | tf_op jit(solution)/shard_map/reduce_scatter | solution.py:22
  890.8 410.9 %all-reduce.3.cloned.1.call-done = f32[256,256]{1,0:T(8,128)} async-done(((f32[256,256]{1,0:T(8,128)}), f32[256,256]{1,0:T(8,128)}) %all-reduce.3.cloned.1.call-update) | async-done | bytes 262160 | tf_op jit(solution)/shard_map/psum | solution.py:40
  1301.7 89.6 %all-reduce.5.cloned.1.call-done = f32[256,256]{1,0:T(8,128)} async-done(((f32[256,256]{1,0:T(8,128)}), f32[256,256]{1,0:T(8,128)}) %all-reduce.5.cloned.1.call-update) | async-done | bytes 262160 | tf_op jit(solution)/shard_map/psum | solution.py:40
  1391.4 1.7 broadcast_multiply_fusion
  (46 shorter events, 7.0 us)
Async XLA Ops:
  7.2 106.7 %all-gather.7.cloned.1.call-start = ((), (), s32[]{:S(2)}) async-start(), calls=%async_computation.6 | async-start | bytes 3244032 | tf_op jit(solution)/shard_map/all_gather | solution.py:18
  7.9 149.8 %copy-start = (f32[96,256]{1,0:T(8,128)S(1)}, f32[96,256]{1,0:T(8,128)}, u32[]{:S(2)}) copy-start(f32[96,256]{1,0:T(8,128)} %param.3) | copy-start | bytes 294916
  7.9 149.8 %reduce-scatter.7.cloned.1.call-start = ((), (), s32[]{:S(2)}) async-start(), calls=%async_computation.7 | async-start | bytes 884736 | tf_op jit(solution)/shard_map/reduce_scatter | solution.py:22
  125.3 134.7 %all-gather.9.cloned.1.call-start = ((), (), s32[]{:S(2)}) async-start(), calls=%async_computation.8 | async-start | bytes 3244032 | tf_op jit(solution)/shard_map/all_gather | solution.py:18
  159.3 144.6 %copy-start.6 = (f32[96,256]{1,0:T(8,128)S(1)}, f32[96,256]{1,0:T(8,128)}, u32[]{:S(2)}) copy-start(f32[96,256]{1,0:T(8,128)} %reduce-scatter.7.cloned.1.call-done) | copy-start | bytes 294916
  159.3 144.6 %reduce-scatter.9.cloned.1.call-start = ((), (), s32[]{:S(2)}) async-start(), calls=%async_computation.9 | async-start | bytes 884736 | tf_op jit(solution)/shard_map/reduce_scatter | solution.py:22
  271.5 134.6 %all-gather.11.cloned.1.call-start = ((), (), s32[]{:S(2)}) async-start(), calls=%async_computation.10 | async-start | bytes 3244032 | tf_op jit(solution)/shard_map/all_gather | solution.py:18
  305.5 144.5 %copy-start.3 = (f32[96,256]{1,0:T(8,128)S(1)}, f32[96,256]{1,0:T(8,128)}, u32[]{:S(2)}) copy-start(f32[96,256]{1,0:T(8,128)} %multiply_subtract_fusion.4) | copy-start | bytes 294916
  305.5 144.5 %reduce-scatter.11.cloned.1.call-start = ((), (), s32[]{:S(2)}) async-start(), calls=%async_computation.11 | async-start | bytes 884736 | tf_op jit(solution)/shard_map/reduce_scatter | solution.py:22
  417.6 134.8 %all-gather.13.cloned.1.call-start = ((), (), s32[]{:S(2)}) async-start(), calls=%async_computation.12 | async-start | bytes 3244032 | tf_op jit(solution)/shard_map/all_gather | solution.py:18
  451.6 144.6 %copy-start.1 = (f32[96,256]{1,0:T(8,128)S(1)}, f32[96,256]{1,0:T(8,128)}, u32[]{:S(2)}) copy-start(f32[96,256]{1,0:T(8,128)} %multiply_subtract_fusion.3) | copy-start | bytes 294916
  451.6 144.6 %reduce-scatter.13.cloned.1.call-start = ((), (), s32[]{:S(2)}) async-start(), calls=%async_computation.13 | async-start | bytes 884736 | tf_op jit(solution)/shard_map/reduce_scatter | solution.py:22
  563.8 134.8 %all-gather.15.cloned.1.call-start = ((), (), s32[]{:S(2)}) async-start(), calls=%async_computation.14 | async-start | bytes 3244032 | tf_op jit(solution)/shard_map/all_gather | solution.py:18
  597.8 144.7 %copy-start.2 = (f32[96,256]{1,0:T(8,128)S(1)}, f32[96,256]{1,0:T(8,128)}, u32[]{:S(2)}) copy-start(f32[96,256]{1,0:T(8,128)} %multiply_subtract_fusion.2) | copy-start | bytes 294916
  597.8 144.7 %reduce-scatter.15.cloned.1.call-start = ((), (), s32[]{:S(2)}) async-start(), calls=%async_computation.15 | async-start | bytes 884736 | tf_op jit(solution)/shard_map/reduce_scatter | solution.py:22
  710.1 134.7 %all-gather.17.cloned.1.call-start = ((), (), s32[]{:S(2)}) async-start(), calls=%async_computation.16 | async-start | bytes 3244032 | tf_op jit(solution)/shard_map/all_gather | solution.py:18
  744.1 144.6 %copy-start.5 = (f32[96,256]{1,0:T(8,128)S(1)}, f32[96,256]{1,0:T(8,128)}, u32[]{:S(2)}) copy-start(f32[96,256]{1,0:T(8,128)} %multiply_subtract_fusion.1) | copy-start | bytes 294916
  744.1 144.6 %reduce-scatter.17.cloned.1.call-start = ((), (), s32[]{:S(2)}) async-start(), calls=%async_computation.17 | async-start | bytes 884736 | tf_op jit(solution)/shard_map/reduce_scatter | solution.py:22
  856.3 445.4 %all-reduce.3.cloned.1.call-start = ((), (), s32[]{:S(2)}) async-start(), calls=%async_computation.18 | async-start | bytes 524288 | tf_op jit(solution)/shard_map/psum | solution.py:40
  889.6 503.5 %copy-start.4 = (f32[96,256]{1,0:T(8,128)}, f32[96,256]{1,0:T(8,128)S(1)}, u32[]{:S(2)}) copy-start(f32[96,256]{1,0:T(8,128)S(1)} %multiply_subtract_fusion) | copy-start | bytes 294916
  890.8 500.6 %all-reduce.5.cloned.1.call-start = ((), (), s32[]{:S(2)}) async-start(), calls=%async_computation.19 | async-start | bytes 524288 | tf_op jit(solution)/shard_map/psum | solution.py:40
Sparse Core Ops, SparseCore 0:
  11.4 102.4 all-gather.6
  125.4 32.2 reduce-scatter.6
  161.7 98.3 all-gather.8
  271.6 32.2 reduce-scatter.8
  307.7 98.3 all-gather.10
  417.7 32.2 reduce-scatter.10
  454.0 98.3 all-gather.12
  564.0 32.2 reduce-scatter.12
  600.2 98.3 all-gather.14
  710.2 32.2 reduce-scatter.14
  746.5 98.3 all-gather.16
  856.4 32.2 reduce-scatter.16
  891.9 409.8 all-reduce.2
  1304.2 87.1 all-reduce.4
